TPU v7x, 512 devices: a whole 4x4x16 slice. The times are simulated.
512 devices in a mesh: req: 32 (over z, core), mlp: 16 (over y, x).
Axes of the slice: x: 4, y: 4, z: 16, core: 2. Of those that a mesh axis runs over, the one named last changes fastest.
Arguments:
- hidden_input: bfloat16 [12288, 4096], P('req', 'mlp'), may hold values from -6 to 6
- input_norm_gain: bfloat16 [4096], replicated, may hold values from 0.099609375 to 1.8984375
- query_norm_gain: bfloat16 [128], replicated, may hold values from 0.099609375 to 1.8984375
- key_norm_gain: bfloat16 [128], replicated, may hold values from 0.099609375 to 1.8984375
- query_weight: bfloat16 [4096, 4096], P('req', 'mlp'), may hold values from -0.09375 to 0.09375
- key_value_weight: bfloat16 [4096, 2, 1024], P('req'), may hold values from -0.09375 to 0.09375
- output_weight: bfloat16 [4096, 16, 256], P('mlp', None, 'req'), may hold values from -0.09375 to 0.09375
- adapter_down_qkv: bfloat16 [64, 48, 4096], P('req', None, 'mlp'), may hold values from -0.09375 to 0.09375
- adapter_down_output: bfloat16 [64, 16, 4096], P('req', None, 'mlp'), may hold values from -0.09375 to 0.09375
- adapter_up_query: bfloat16 [64, 16, 4096], P('req', None, 'mlp'), may hold values from -1.5 to 1.5
- adapter_up_key_value: bfloat16 [64, 16, 2, 1024], P('req'), may hold values from -1.5 to 1.5
- adapter_up_output: bfloat16 [64, 16, 4096], P('req', None, 'mlp'), may hold values from -1.5 to 1.5
- pool: bfloat16 [16384, 2, 1024], P('req'), may hold values from -6 to 6
- lengths: int32 [32, 4], P('req'), may hold values from 1 to 192, 384 in all within a row
- cached_prefix_pages: int32 [32, 4], P('req'), may hold values from 0 to 8
- prefix_page_table: int32 [32, 4, 8], P('req'), may hold values from 0 to 7, each once within a row
- adapter_of_request: int32 [32, 4, 1], P('req'), may hold values from 0 to 63
- adapter_storage: int32 [64], replicated, may hold values from 0 to 63, each once
Outputs:
- attention_update: bfloat16 [12288, 4096], P('req', 'mlp')
- new_cache: bfloat16 [12288, 2, 1024], P('req', None, 'mlp')
Inputs may be any that keep to these rules, and one draw needn't show every extreme that they name: The lengths of one index of req sum to 384, and the longest of them is 192. `prefix_page_table`: each row lists every page of its pool once. `adapter_of_request`: every adapter is used by some request. `adapter_storage`: each slot holds one adapter.
All inputs are finite; a program needn't handle non-finite values.
Results may differ from a plain program's by a relative error of at most 0.035.
Values may be sent and summed in bfloat16 or wider, within the bound.
A program may use at most 64 MiB of HBM per device.

v0:
```python
import math
import jax
import jax.numpy as jnp
from jax import lax
from jax.sharding import PartitionSpec as P

QUERY_HEADS = 32
KEY_VALUE_HEADS = 8
HEAD_SIZE = 128
ADAPTER_RANK = 16
PAGE = 64
epsilon = 1e-06
rope_base = 1000000.0


def root_mean_scale(values, gain_vec):
    mean_sq = jnp.mean(values * values, axis=-1, keepdims=True)
    return values * lax.rsqrt(mean_sq + epsilon) * gain_vec.astype(jnp.float32)


def rotary_embed(values, token_positions):
    half_width = values.shape[-1] // 2
    inverse_freq = jnp.exp(
        jnp.arange(half_width, dtype=jnp.float32) * (-2.0 / values.shape[-1]) * math.log(rope_base)
    )
    angles = token_positions.astype(jnp.float32)[:, None] * inverse_freq[None, :]
    cosine = jnp.cos(angles)[:, None, :]
    sine_part = jnp.sin(angles)[:, None, :]
    front = values[..., :half_width]
    back = values[..., half_width:]
    return jnp.concatenate(
        [front * cosine - back * sine_part, back * cosine + front * sine_part], axis=-1
    )


def row_tables(lengths_row, prefix_row, page_rows, row_count):
    ends_at = jnp.cumsum(lengths_row)
    starts_at = ends_at - lengths_row
    row_ids = jnp.arange(row_count, dtype=jnp.int32)
    owners = jnp.sum((row_ids[:, None] >= ends_at[None, :]).astype(jnp.int32), axis=1)
    group_members = owners[:, None] == jnp.arange(lengths_row.shape[0], dtype=jnp.int32)[None, :]
    offsets = PAGE * prefix_row[None, :] + row_ids[:, None] - starts_at[None, :]
    token_positions = jnp.sum(jnp.where(group_members, offsets, 0), axis=1)
    page_ids = jnp.arange(page_rows.shape[1], dtype=jnp.int32)
    listed = (page_rows[:, :, None] == page_ids[None, None, :]) & (
        page_ids[None, :, None] < prefix_row[:, None, None]
    )
    page_used = jnp.sum(listed.astype(jnp.float32), axis=1)
    return (owners, group_members, token_positions, page_used)


def apply_adapter(lowrank_inner, group_members, chosen_up):
    masked = lowrank_inner[:, None, :] * group_members.astype(lowrank_inner.dtype)[:, :, None]
    return jnp.einsum("gjr,jrc->gc", masked, chosen_up, preferred_element_type=jnp.float32)


def select_rows(terms, group_members):
    return jnp.sum(terms * group_members.astype(jnp.float32)[:, :, None], axis=1)


def shards(
    hidden_input,
    input_norm_gain,
    query_norm_gain,
    key_norm_gain,
    query_weight,
    key_value_weight,
    output_weight,
    adapter_down_qkv,
    adapter_down_output,
    adapter_up_query,
    adapter_up_key_value,
    adapter_up_output,
    pool,
    lengths,
    cached_prefix_pages,
    prefix_page_table,
    adapter_of_request,
    adapter_storage,
):
    feature_group_count = lax.axis_size("mlp")
    feature_group_index = lax.axis_index("mlp")
    whole = lax.all_gather(hidden_input, "mlp", axis=1, tiled=True)
    row_count, full_width = whole.shape
    normalized_input = root_mean_scale(whole.astype(jnp.float32), input_norm_gain).astype(
        jnp.bfloat16
    )
    owners, group_members, token_positions, page_used = row_tables(
        lengths[0], cached_prefix_pages[0], prefix_page_table[0], row_count
    )
    q_width = query_weight.shape[1]
    query_head_rows = q_width // HEAD_SIZE
    key_value_local = max(1, KEY_VALUE_HEADS // feature_group_count)
    key_value_width = key_value_local * HEAD_SIZE
    key_value_begin = (
        feature_group_index * query_head_rows // (QUERY_HEADS // KEY_VALUE_HEADS) * HEAD_SIZE
    )
    own_wkv = lax.dynamic_slice_in_dim(key_value_weight, key_value_begin, key_value_width, 2)
    request_key_value_up = lax.dynamic_slice_in_dim(
        adapter_up_key_value, key_value_begin, key_value_width, 3
    )
    gathered = (
        lax.all_gather(adapter_down_qkv, "req", axis=0, tiled=True),
        lax.all_gather(adapter_down_output, "req", axis=0, tiled=True),
        lax.all_gather(adapter_up_query, "req", axis=0, tiled=True),
        lax.all_gather(request_key_value_up, "req", axis=0, tiled=True),
        lax.all_gather(adapter_up_output, "req", axis=0, tiled=True),
    )
    slot_indices = jnp.take(adapter_storage, adapter_of_request[0, :, 0], axis=0)
    chosen_down = jnp.take(gathered[0], slot_indices, axis=0)
    output_down = jnp.take(gathered[1], slot_indices, axis=0)
    query_up_part = jnp.take(gathered[2], slot_indices, axis=0)
    key_value_up = jnp.take(gathered[3], slot_indices, axis=0)
    output_up = jnp.take(gathered[4], slot_indices, axis=0)
    feature_cols = full_width // feature_group_count
    own_normed = lax.dynamic_slice_in_dim(
        normalized_input, feature_group_index * feature_cols, feature_cols, 1
    )
    low_terms = jnp.einsum(
        "gd,jkd->gjk", own_normed, chosen_down, preferred_element_type=jnp.float32
    )
    lowrank_inner = lax.psum(select_rows(low_terms, group_members).astype(jnp.bfloat16), "mlp")
    q_part = lax.all_gather(query_weight, "req", axis=0, tiled=True)
    kv_part = lax.all_gather(own_wkv, "req", axis=0, tiled=True)
    query_width_total = jnp.dot(normalized_input, q_part, preferred_element_type=jnp.float32)
    kv_total = jnp.dot(
        normalized_input,
        kv_part.reshape(kv_part.shape[0], 2 * key_value_width),
        preferred_element_type=jnp.float32,
    )
    query_width_total, kv_total = (query_width_total, kv_total)
    query_plain = (
        query_width_total
        + apply_adapter(lowrank_inner[:, 0:ADAPTER_RANK], group_members, query_up_part)
    ).astype(jnp.bfloat16)
    key_lowrank_part = apply_adapter(
        lowrank_inner[:, ADAPTER_RANK : 2 * ADAPTER_RANK], group_members, key_value_up[:, :, 0]
    )
    value_lowrank_part = apply_adapter(
        lowrank_inner[:, 2 * ADAPTER_RANK : 3 * ADAPTER_RANK], group_members, key_value_up[:, :, 1]
    )
    key_value_plain = (
        kv_total.reshape(row_count, 2, key_value_width)
        + jnp.stack([key_lowrank_part, value_lowrank_part], axis=1)
    ).astype(jnp.bfloat16)
    cached = lax.dynamic_slice_in_dim(pool, key_value_begin, key_value_width, 2)
    pool_token_rows = cached.shape[0]
    query_rotated = rotary_embed(
        root_mean_scale(
            query_plain.astype(jnp.float32).reshape(row_count, query_head_rows, HEAD_SIZE),
            query_norm_gain,
        ),
        token_positions,
    ).astype(jnp.bfloat16)
    key_rotated = rotary_embed(
        root_mean_scale(
            key_value_plain[:, 0]
            .astype(jnp.float32)
            .reshape(row_count, key_value_local, HEAD_SIZE),
            key_norm_gain,
        ),
        token_positions,
    ).astype(jnp.bfloat16)
    cache_columns = KEY_VALUE_HEADS * HEAD_SIZE // feature_group_count
    own_offset = feature_group_index * cache_columns - key_value_begin
    local_cache = jnp.stack(
        [key_rotated.reshape(row_count, key_value_width), key_value_plain[:, 1]], axis=1
    )
    new_cache = lax.dynamic_slice_in_dim(local_cache, own_offset, cache_columns, 2)
    key_matrix = jnp.concatenate(
        [cached[:, 0].reshape(pool_token_rows, key_value_local, HEAD_SIZE), key_rotated], axis=0
    )
    value_matrix = jnp.concatenate(
        [
            cached[:, 1].reshape(pool_token_rows, key_value_local, HEAD_SIZE),
            key_value_plain[:, 1].reshape(row_count, key_value_local, HEAD_SIZE),
        ],
        axis=0,
    )
    pool_ok = jnp.dot(group_members.astype(jnp.float32), page_used, precision=lax.Precision.HIGHEST)
    pool_ok = jnp.repeat(pool_ok, PAGE, axis=1) > 0.5
    row_ids = jnp.arange(row_count, dtype=jnp.int32)
    causal = (owners[:, None] == owners[None, :]) & (row_ids[None, :] <= row_ids[:, None])
    allowed = jnp.concatenate([pool_ok, causal], axis=1)
    query_rows = query_rotated.reshape(
        row_count, key_value_local, query_head_rows // key_value_local, HEAD_SIZE
    )
    scores = jnp.einsum(
        "gkhd,skd->khgs", query_rows, key_matrix, preferred_element_type=jnp.float32
    ) / math.sqrt(HEAD_SIZE)
    exp_scores = jnp.where(allowed[None, None], jnp.exp(scores), 0.0)
    softmax = (exp_scores / jnp.sum(exp_scores, axis=-1, keepdims=True)).astype(jnp.bfloat16)
    attended = jnp.einsum(
        "khgs,skd->gkhd", softmax, value_matrix, preferred_element_type=jnp.float32
    )
    attended = attended.astype(jnp.bfloat16).reshape(row_count, q_width)
    out_terms = jnp.einsum("gc,jrc->gjr", attended, output_down, preferred_element_type=jnp.float32)
    lowrank_result = lax.psum(select_rows(out_terms, group_members), "mlp").astype(jnp.bfloat16)
    partial_value = jnp.einsum(
        "gc,cnk->gnk",
        attended,
        lax.all_gather(output_weight, "req", axis=2, tiled=True),
        preferred_element_type=jnp.float32,
    )
    summed_output = lax.psum_scatter(
        partial_value.reshape(row_count, full_width).astype(jnp.bfloat16),
        "mlp",
        scatter_dimension=1,
        tiled=True,
    ).astype(jnp.float32)
    attention_update = (
        summed_output + apply_adapter(lowrank_result, group_members, output_up)
    ).astype(jnp.bfloat16)
    return (attention_update, new_cache)


def solution(mesh):
    return jax.shard_map(
        shards,
        mesh=mesh,
        in_specs=(
            P("req", "mlp"),
            P(),
            P(),
            P(),
            P("req", "mlp"),
            P("req", None, None),
            P("mlp", None, "req"),
            P("req", None, "mlp"),
            P("req", None, "mlp"),
            P("req", None, "mlp"),
            P("req", None, None, None),
            P("req", None, "mlp"),
            P("req", None, None),
            P("req", None),
            P("req", None),
            P("req", None, None),
            P("req", None, None),
            P(),
        ),
        out_specs=(P("req", "mlp"), P("req", None, "mlp")),
        check_vma=False,
    )
```

profile of v0, /device:TPU:32, one launch (start us, length us, event | category | flops | bytes accessed | tf_op | source)
XLA Modules:
  0.0 518.9 jit_solution(2938642543624137017)
XLA Ops:
  7.3 0.7 all-gather.10.cloned.1.call-update
  8.0 0.2 copy-done
  8.2 0.7 constant_dynamic-slice_fusion.2
  9.0 0.7 all-gather.6.cloned.1.call-update
  9.7 0.5 all-gather.12.cloned.1.call-update
  10.3 0.5 all-gather.14.cloned.1.call-update
  10.9 0.7 fusion.90
  11.6 1.3 gather_fusion
  12.9 0.7 fusion.80
  13.5 0.7 compare_and_fusion
  14.2 0.8 reduce-window.4
  15.0 0.7 fusion.81
  15.8 0.6 fusion.76
  16.4 0.1 fusion.28
  16.5 0.7 constant_dynamic-slice_fusion.1
  17.3 36.1 %all_gather.30 = bf16[64,16,2,128]{3,1,2,0:T(8,128)(2,1)S(1)} all-gather(bf16[2,16,2,128]{3,1,2,0:T(8,128)(2,1)S(1)} %copy.66), channel_id=1, replica_groups=mesh['req'=32,'mlp'=16] {'req'}, dimensions={0}, use_global_device_ids=true | all-gather | bytes 540672 | tf_op jit(solution)/shard_map/all_gather | solution.py:106
  53.3 0.7 convert_element_type.100
  54.0 1.2 convert_element_type.109
  55.2 0.7 multiply_bitcast_fusion
  55.9 0.1 select_reduce_fusion
  56.0 1.6 constant_dynamic-slice_fusion
  57.6 30.2 %all_gather.32 = bf16[64,16,256]{2,1,0:T(8,128)(2,1)S(1)} all-gather(bf16[2,16,256]{2,1,0:T(8,128)(2,1)S(1)} %copy-done.6), channel_id=1, replica_groups=mesh['req'=32,'mlp'=16] {'req'}, dimensions={0}, use_global_device_ids=true | all-gather | bytes 540672 | tf_op jit(solution)/shard_map/all_gather | solution.py:105
  87.8 0.5 convert_element_type.112
  88.4 0.1 convert_reduce_fusion
  88.5 0.2 convolution_compare_fusion
  88.7 0.7 copy.65
  89.4 0.6 gather_fusion.2
  90.0 0.7 copy_select_fusion
  90.7 1.2 gather_fusion.3
  91.8 0.8 multiply_cosine_fusion
  92.8 2.6 gather_fusion.1
  95.4 61.2 %all-gather.8.cloned.1.call-done = bf16[4096,2,128]{2,1,0:T(2,128)(2,1)} async-done(((bf16[128,2,128]{2,1,0:T(2,128)(2,1)}), bf16[4096,2,128]{2,1,0:T(2,128)(2,1)}) %all-gather.8.cloned.1.call-update) | async-done | bytes 2097168 | tf_op jit(solution)/shard_map/all_gather | solution.py:124
  156.6 4.7 copy.61
  161.3 63.1 %all-gather.6.cloned.1.call-done = bf16[384,4096]{1,0:T(8,128)(2,1)} async-done(((bf16[384,256]{1,0:T(8,128)(2,1)}), bf16[384,4096]{1,0:T(8,128)(2,1)}) %all-gather.6.cloned.1.call-update) | async-done | bytes 3145744 | tf_op jit(solution)/shard_map/all_gather | solution.py:83
  224.4 2.7 fusion
  227.2 0.1 copy-done.1
  227.3 1.1 fusion.2
  228.4 1.6 copy-done.2
  230.0 0.9 fusion.26
  230.9 72.8 %psum.14 = bf16[384,48]{0,1:T(8,128)(2,1)S(1)} all-reduce(bf16[384,48]{0,1:T(8,128)(2,1)} %fusion.26), channel_id=1, replica_groups=mesh['req'=32,'mlp'=16] {'mlp'}, use_global_device_ids=true, to_apply=%region_4.5 | all-reduce | flops 18432 | bytes 73728 | tf_op jit(solution)/shard_map/psum | solution.py:122
  303.7 0.9 convolution_bitcast_fusion.2
  304.7 0.9 convolution_bitcast_fusion.3
  305.6 3.2 fusion.17
  309.0 0.4 fusion.46
  309.5 0.1 copy.53
  309.6 3.8 fusion.92
  313.5 0.4 multiply_reduce_fusion
  313.8 0.1 copy.54
  314.0 0.1 copy.52
  314.1 0.2 multiply_multiply_fusion
  314.3 0.2 subtract_convert_fusion
  314.5 0.9 fusion.5
  315.5 0.9 fusion.23
  316.4 53.5 %all-gather.14.cloned.1.call-done = bf16[256,16,256]{0,2,1:T(8,128)(2,1)} async-done(((bf16[256,16,8]{0,2,1:T(8,128)(2,1)}), bf16[256,16,256]{0,2,1:T(8,128)(2,1)}) %all-gather.14.cloned.1.call-update) | async-done | bytes 2097168 | tf_op jit(solution)/shard_map/all_gather | solution.py:202
  369.9 4.3 convolution_convert_fusion
  374.2 0.7 copy-done.7
  374.9 28.9 %all_gather.34 = bf16[64,16,256]{2,1,0:T(8,128)(2,1)S(1)} all-gather(bf16[2,16,256]{2,1,0:T(8,128)(2,1)S(1)} %copy-done.7), channel_id=1, replica_groups=mesh['req'=32,'mlp'=16] {'req'}, dimensions={0}, use_global_device_ids=true | all-gather | bytes 540672 | tf_op jit(solution)/shard_map/all_gather | solution.py:104
  403.8 0.5 gather_fusion.4
  404.3 30.1 %all_gather.35 = bf16[64,16,256]{2,1,0:T(8,128)(2,1)S(1)} all-gather(bf16[2,16,256]{2,1,0:T(8,128)(2,1)S(1)} %copy-done.8), channel_id=1, replica_groups=mesh['req'=32,'mlp'=16] {'req'}, dimensions={0}, use_global_device_ids=true | all-gather | bytes 540672 | tf_op jit(solution)/shard_map/all_gather | solution.py:107
  434.4 0.5 gather_fusion.5
  435.0 0.2 fusion.27
  435.2 74.3 %psum.15 = bf16[384,16]{0,1:T(8,128)(2,1)S(1)} all-reduce(f32[384,16]{0,1:T(8,128)S(1)} %fusion.27), channel_id=1, replica_groups=mesh['req'=32,'mlp'=16] {'mlp'}, use_global_device_ids=true, to_apply=%region_12.14 | all-reduce | flops 6144 | bytes 36864 | tf_op jit(solution)/shard_map/psum | solution.py:198
  509.5 0.7 fusion.50
  510.2 1.9 fusion.16
  (62 shorter events, 0.9 us)
Async XLA Ops:
  7.2 1.1 copy-start
  7.2 81.2 %copy-start.17 = (s32[1,4]{1,0:T(1,128)S(1)}, s32[1,4]{1,0:T(1,128)}, u32[]{:S(2)}) copy-start(s32[1,4]{1,0:T(1,128)} %param.34) | copy-start | bytes 52
  7.2 50.4 %copy-start.6 = (bf16[2,16,256]{2,1,0:T(8,128)(2,1)S(1)}, bf16[2,16,256]{2,1,0:T(8,128)(2,1)}, u32[]{:S(2)}) copy-start(bf16[2,16,256]{2,1,0:T(8,128)(2,1)} %param.29) | copy-start | bytes 49156
  7.2 80.6 %copy-start.16 = (bf16[128]{0:T(256)(128)(2,1)S(1)}, bf16[128]{0:T(256)(128)(2,1)}, u32[]{:S(2)}) copy-start(bf16[128]{0:T(256)(128)(2,1)} %param.22) | copy-start | bytes 772
  7.2 81.2 %copy-start.13 = (s32[1,4,8]{2,1,0:T(4,128)S(1)}, s32[1,4,8]{2,1,0:T(4,128)}, u32[]{:S(2)}) copy-start(s32[1,4,8]{2,1,0:T(4,128)} %param.35) | copy-start | bytes 388
  7.2 85.5 %all-gather.10.cloned.1.call-start = ((), (), s32[]{:S(2)}) async-start(), calls=%async_computation.3 | async-start | bytes 1622016 | tf_op jit(solution)/shard_map/all_gather | solution.py:103
  8.0 148.6 %all-gather.8.cloned.1.call-start = ((), (), s32[]{:S(2)}) async-start(), calls=%async_computation.2 | async-start | bytes 2162688 | tf_op jit(solution)/shard_map/all_gather | solution.py:124
  8.9 215.5 %all-gather.6.cloned.1.call-start = ((), (), s32[]{:S(2)}) async-start(), calls=%async_computation.1 | async-start | bytes 3342336 | tf_op jit(solution)/shard_map/all_gather | solution.py:83
  9.7 299.9 %all-gather.12.cloned.1.call-start = ((), (), s32[]{:S(2)}) async-start(), calls=%async_computation.4 | async-start | bytes 2162688 | tf_op jit(solution)/shard_map/all_gather | solution.py:123
  10.3 359.6 %all-gather.14.cloned.1.call-start = ((), (), s32[]{:S(2)}) async-start(), calls=%async_computation.5 | async-start | bytes 2162688 | tf_op jit(solution)/shard_map/all_gather | solution.py:202
  10.8 499.4 %reduce-scatter.2.cloned.1.call-start = ((), (), s32[]{:S(2)}) async-start(), calls=%async_computation.6 | async-start | bytes 3342336 | tf_op jit(solution)/shard_map/reduce_scatter | solution.py:205
  14.2 147.1 %copy-start.11 = (f32[64]{0:T(128)}, f32[64]{0:T(128)S(1)}, u32[]{:S(2)}) copy-start(f32[64]{0:T(128)S(1)} %multiply_exponential_fusion) | copy-start | bytes 772
  224.4 2.8 copy-start.1
  227.3 2.8 copy-start.5
  227.3 2.8 copy-start.9
  228.4 1.7 copy-start.2
  305.6 3.3 copy-start.14
  305.6 3.4 copy-start.12
  309.6 3.9 copy-start.4
  309.6 4.5 copy-start.15
  314.3 1.2 copy-start.3
  374.1 0.7 copy-start.7
  374.1 30.2 %copy-start.8 = (bf16[2,16,256]{2,1,0:T(8,128)(2,1)S(1)}, bf16[2,16,256]{2,1,0:T(8,128)(2,1)}, u32[]{:S(2)}) copy-start(bf16[2,16,256]{2,1,0:T(8,128)(2,1)} %param.31) | copy-start | bytes 49156
  374.1 60.9 %copy-start.10 = (f32[384,4]{0,1:T(4,128)S(1)}, f32[384,4]{0,1:T(4,128)}, u32[]{:S(2)}) copy-start(f32[384,4]{0,1:T(4,128)} %get-tuple-element.17) | copy-start | bytes 18436
Sparse Core Ops, SparseCore 0:
  10.2 75.3 all-gather.9
  87.7 68.8 all-gather.7
  159.6 64.8 all-gather.5
  226.4 71.1 all-gather.11
  299.5 70.3 all-gather.13
  374.3 87.2 reduce-scatter.1
where the time goes:
time: 520 us; the launch traced here: 519 us
  blocking collectives  272 us (52%)
  waiting for transfers between devices  180 us (35%)
  matrix products  18.5 us (4%)
  local copies, waits for them, and re-layouts  18.3 us (4%)
  other arithmetic  14.7 us (3%)
  between operations  14.6 us (3%)
    psum x1, blocking collectives, shards(): lax.psum(select_rows(out_terms, group_members), 'mlp').astype(jnp.bfloat16)  74.3 us
    psum x1, blocking collectives, shards(): lax.psum(select_rows(low_terms, group_members).astype(jnp.bfloat16), 'mlp')  72.8 us
    all_gather x1, waiting for transfers between devices, shards(): whole = lax.all_gather(hidden_input, 'mlp', axis=1, tiled=True)  63.1 us
    all_gather x1, waiting for transfers between devices, shards(): kv_part = lax.all_gather(own_wkv, 'req', axis=0, tiled=True)  61.2 us
    all_gather x1, waiting for transfers between devices, shards(): lax.all_gather(output_weight, 'req', axis=2, tiled=True)  53.5 us
    all_gather x1, blocking collectives, shards(): lax.all_gather(request_key_value_up, 'req', axis=0, tiled=True)  36.1 us
    all_gather x1, blocking collectives, shards(): lax.all_gather(adapter_up_query, 'req', axis=0, tiled=True)  30.2 us
    all_gather x1, blocking collectives, shards(): lax.all_gather(adapter_up_output, 'req', axis=0, tiled=True)  30.1 us
  transfers between devices with their start and end apart: 6, of which 3 were waited for; matrix products, arithmetic and copies ran while one was open for 8% of the time, Pallas kernels for 0%

commit v1 on v0

--- a/solution.py
+++ b/solution.py
@@ -11,6 +11,24 @@
 PAGE = 64
 epsilon = 1e-06
 rope_base = 1000000.0
+
+
+def ring_gather(shard, axis, dim):
+    ways, here, hop = (lax.axis_size(axis), lax.axis_index(axis), shard.shape[dim])
+    lengths = [n * ways if d == dim else n for d, n in enumerate(shard.shape)]
+    full = lax.dynamic_update_slice_in_dim(
+        jnp.zeros(lengths, shard.dtype), shard, here * hop, axis=dim
+    )
+    going_up = going_down = shard
+    for far in range(1, ways // 2 + 1):
+        going_up = lax.ppermute(going_up, axis, [(d, (d + 1) % ways) for d in range(ways)])
+        full = lax.dynamic_update_slice_in_dim(full, going_up, (here - far) % ways * hop, axis=dim)
+        if 2 * far < ways:
+            going_down = lax.ppermute(going_down, axis, [(d, (d - 1) % ways) for d in range(ways)])
+            full = lax.dynamic_update_slice_in_dim(
+                full, going_down, (here + far) % ways * hop, axis=dim
+            )
+    return full
 
 
 def root_mean_scale(values, gain_vec):
@@ -80,7 +98,7 @@
 ):
     feature_group_count = lax.axis_size("mlp")
     feature_group_index = lax.axis_index("mlp")
-    whole = lax.all_gather(hidden_input, "mlp", axis=1, tiled=True)
+    whole = ring_gather(hidden_input, "mlp", 1)
     row_count, full_width = whole.shape
     normalized_input = root_mean_scale(whole.astype(jnp.float32), input_norm_gain).astype(
         jnp.bfloat16

time: 520 us -> 450 us (0.87)
  waiting for transfers between devices: 180 us -> 32.3 us
  starting transfers between devices: 0.23 us -> 66.2 us
  local copies, waits for them, and re-layouts: 18.3 us -> 29.2 us
    ppermute x0 -> x15, starting transfers between devices: none -> 66 us  [the longest x7 49.2 us: ring_gather(): lax.ppermute(going_down, axis, [(d, (d - 1) % ways) for d in range(ways)])]
    all_gather x1 -> x0, waiting for transfers between devices: 63.1 us -> none  [shards(): whole = lax.all_gather(hidden_input, 'mlp', axis=1, tiled=True)]
    all_gather x1, waiting for transfers between devices: 61.2 us -> 0.01 us  [shards(): kv_part = lax.all_gather(own_wkv, 'req', axis=0, tiled=True)]
    all_gather x1, waiting for transfers between devices: 53.5 us -> 19.6 us  [shards(): lax.all_gather(output_weight, 'req', axis=2, tiled=True)]
    dynamic_update_slice x0 -> x16, local copies, waits for them, and re-layouts: none -> 11.5 us  [the longest x8 5.73 us: ring_gather(): lax.dynamic_update_slice_in_dim(full, going_up, (here - far) % ways * hop...]
    ppermute x0 -> x15, waiting for transfers between devices: none -> 11.3 us  [the longest x8 11.2 us: ring_gather(): lax.ppermute(going_up, axis, [(d, (d + 1) % ways) for d in range(ways)])]
  transfers between devices with their start and end apart: 6 -> 20, of which waited for: 3 -> 8; matrix products, arithmetic and copies ran while one was open for 8% -> 13% of each run, Pallas kernels for 0% -> 0%
where the time goes in v1:
time: 450 us; the launch traced here: 449 us
  blocking collectives  270 us (60%)
  starting transfers between devices  66.2 us (15%)
  waiting for transfers between devices  32.3 us (7%)
  local copies, waits for them, and re-layouts  29.2 us (6%)
  matrix products  18.9 us (4%)
  other arithmetic  18.3 us (4%)
  between operations  14.6 us (3%)
    psum x1, blocking collectives, shards(): lax.psum(select_rows(out_terms, group_members), 'mlp').astype(jnp.bfloat16)  74.3 us
    psum x1, blocking collectives, shards(): lax.psum(select_rows(low_terms, group_members).astype(jnp.bfloat16), 'mlp')  69.8 us
    ppermute x7, starting transfers between devices, ring_gather(): lax.ppermute(going_down, axis, [(d, (d - 1) % ways) for d in range(ways)])  49.2 us
    all_gather x1, blocking collectives, shards(): lax.all_gather(request_key_value_up, 'req', axis=0, tiled=True)  35.8 us
    all_gather x1, blocking collectives, shards(): lax.all_gather(adapter_up_query, 'req', axis=0, tiled=True)  30.8 us
    all_gather x1, blocking collectives, shards(): lax.all_gather(adapter_up_output, 'req', axis=0, tiled=True)  30 us
    all_gather x1, blocking collectives, shards(): lax.all_gather(adapter_down_output, 'req', axis=0, tiled=True)  29.1 us
    all_gather x1, waiting for transfers between devices, shards(): lax.all_gather(output_weight, 'req', axis=2, tiled=True)  19.6 us
  transfers between devices with their start and end apart: 20, of which 8 were waited for; matrix products, arithmetic and copies ran while one was open for 13% of the time, Pallas kernels for 0%

profile of v1, /device:TPU:32, one launch (start us, length us, event | category | flops | bytes accessed | tf_op | source)
XLA Modules:
  0.0 449.2 jit_solution(9763253592710654498)
XLA Ops:
  9.7 3.4 collective-permute-start
  13.1 5.8 %collective-permute-start.1 = (bf16[384,256]{1,0:T(8,128)(2,1)}, bf16[384,256]{1,0:T(8,128)(2,1)S(1)}, u32[]{:S(2)}, u32[]{:S(2)}) collective-permute-start(bf16[384,256]{1,0:T(8,128)(2,1)} %param.20), channel_id=1, source_target_pairs={{0,15},{1,0},{2,1},{3,2},{4,3},{5,4},{6,5},{7,6},{8,7},{9,8},{10,9... | collective-permute-start | bytes 589832 | tf_op jit(solution)/shard_map/ppermute | solution.py:27
  19.9 1.3 gather_fusion
  23.2 0.8 reduce-window.4
  24.8 0.7 constant_dynamic-slice_fusion.1
  25.6 35.8 %all_gather.26 = bf16[64,16,2,128]{3,1,2,0:T(8,128)(2,1)S(1)} all-gather(bf16[2,16,2,128]{3,1,2,0:T(8,128)(2,1)S(1)} %copy.66), channel_id=1, replica_groups=mesh['req'=32,'mlp'=16] {'req'}, dimensions={0}, use_global_device_ids=true | all-gather | bytes 540672 | tf_op jit(solution)/shard_map/all_gather | solution.py:124
  61.3 1.2 convert_element_type.109
  63.5 30.8 %all_gather.28 = bf16[64,16,256]{2,1,0:T(8,128)(2,1)S(1)} all-gather(bf16[2,16,256]{2,1,0:T(8,128)(2,1)} %param.29), channel_id=1, replica_groups=mesh['req'=32,'mlp'=16] {'req'}, dimensions={0}, use_global_device_ids=true | all-gather | bytes 540672 | tf_op jit(solution)/shard_map/all_gather | solution.py:123
  94.3 1.2 convert_element_type.112
  95.5 1.6 constant_dynamic-slice_fusion
  98.3 2.0 broadcast_in_dim.47
  100.3 0.8 constant_dynamic-update-slice_fusion.15
  102.3 0.8 multiply_cosine_fusion
  103.1 0.8 pad_add_fusion
  103.9 1.9 collective-permute-start.2
  105.8 7.2 %collective-permute-start.3 = (bf16[384,256]{1,0:T(8,128)(2,1)S(1)}, bf16[384,256]{1,0:T(8,128)(2,1)S(1)}, u32[]{:S(2)}, u32[]{:S(2)}) collective-permute-start(bf16[384,256]{1,0:T(8,128)(2,1)S(1)} %collective-permute-done.1), channel_id=1, source_target_pairs={{0,15},{1,0},{2,1},{3,2},{4,3},{5,4},{6,5},{7,6},{8,7},{9,8},{10,9... | collective-permute-start | bytes 589832 | tf_op jit(solution)/shard_map/ppermute | solution.py:27
  113.1 0.7 constant_dynamic-update-slice_fusion.14
  113.8 0.7 constant_dynamic-update-slice_fusion.13
  114.5 1.7 collective-permute-done.2
  116.3 1.9 collective-permute-start.4
  118.2 7.2 %collective-permute-start.5 = (bf16[384,256]{1,0:T(8,128)(2,1)S(1)}, bf16[384,256]{1,0:T(8,128)(2,1)S(1)}, u32[]{:S(2)}, u32[]{:S(2)}) collective-permute-start(bf16[384,256]{1,0:T(8,128)(2,1)S(1)} %collective-permute-done.3), channel_id=1, source_target_pairs={{0,15},{1,0},{2,1},{3,2},{4,3},{5,4},{6,5},{7,6},{8,7},{9,8},{10,9... | collective-permute-start | bytes 589832 | tf_op jit(solution)/shard_map/ppermute | solution.py:27
  125.4 0.7 constant_dynamic-update-slice_fusion.12
  126.2 0.7 constant_dynamic-update-slice_fusion.11
  126.9 0.9 collective-permute-done.4
  127.8 1.9 collective-permute-start.6
  129.8 7.2 %collective-permute-start.7 = (bf16[384,256]{1,0:T(8,128)(2,1)S(1)}, bf16[384,256]{1,0:T(8,128)(2,1)S(1)}, u32[]{:S(2)}, u32[]{:S(2)}) collective-permute-start(bf16[384,256]{1,0:T(8,128)(2,1)S(1)} %collective-permute-done.5), channel_id=1, source_target_pairs={{0,15},{1,0},{2,1},{3,2},{4,3},{5,4},{6,5},{7,6},{8,7},{9,8},{10,9... | collective-permute-start | bytes 589832 | tf_op jit(solution)/shard_map/ppermute | solution.py:27
  137.0 0.7 constant_dynamic-update-slice_fusion.10
  137.7 0.7 constant_dynamic-update-slice_fusion.9
  138.7 1.9 collective-permute-start.8
  140.6 7.2 %collective-permute-start.9 = (bf16[384,256]{1,0:T(8,128)(2,1)S(1)}, bf16[384,256]{1,0:T(8,128)(2,1)S(1)}, u32[]{:S(2)}, u32[]{:S(2)}) collective-permute-start(bf16[384,256]{1,0:T(8,128)(2,1)S(1)} %collective-permute-done.7), channel_id=1, source_target_pairs={{0,15},{1,0},{2,1},{3,2},{4,3},{5,4},{6,5},{7,6},{8,7},{9,8},{10,9... | collective-permute-start | bytes 589832 | tf_op jit(solution)/shard_map/ppermute | solution.py:27
  147.9 0.7 constant_dynamic-update-slice_fusion.8
  148.6 0.7 constant_dynamic-update-slice_fusion.7
  149.6 1.9 collective-permute-start.10
  151.5 7.2 %collective-permute-start.11 = (bf16[384,256]{1,0:T(8,128)(2,1)S(1)}, bf16[384,256]{1,0:T(8,128)(2,1)S(1)}, u32[]{:S(2)}, u32[]{:S(2)}) collective-permute-start(bf16[384,256]{1,0:T(8,128)(2,1)S(1)} %collective-permute-done.9), channel_id=1, source_target_pairs={{0,15},{1,0},{2,1},{3,2},{4,3},{5,4},{6,5},{7,6},{8,7},{9,8},{10,9... | collective-permute-start | bytes 589832 | tf_op jit(solution)/shard_map/ppermute | solution.py:27
  158.7 0.7 constant_dynamic-update-slice_fusion.6
  159.5 0.7 constant_dynamic-update-slice_fusion.5
  160.4 1.9 collective-permute-start.12
  162.4 7.2 %collective-permute-start.13 = (bf16[384,256]{1,0:T(8,128)(2,1)S(1)}, bf16[384,256]{1,0:T(8,128)(2,1)S(1)}, u32[]{:S(2)}, u32[]{:S(2)}) collective-permute-start(bf16[384,256]{1,0:T(8,128)(2,1)S(1)} %collective-permute-done.11), channel_id=1, source_target_pairs={{0,15},{1,0},{2,1},{3,2},{4,3},{5,4},{6,5},{7,6},{8,7},{9,8},{10,9... | collective-permute-start | bytes 589832 | tf_op jit(solution)/shard_map/ppermute | solution.py:27
  169.6 0.7 constant_dynamic-update-slice_fusion.4
  170.3 0.7 constant_dynamic-update-slice_fusion.3
  171.3 1.9 collective-permute-start.14
  173.2 0.7 constant_dynamic-update-slice_fusion.2
  173.9 0.7 constant_dynamic-update-slice_fusion.1
  174.7 7.5 %collective-permute-done.14 = bf16[384,256]{1,0:T(8,128)(2,1)S(1)} collective-permute-done((bf16[384,256]{1,0:T(8,128)(2,1)S(1)}, bf16[384,256]{1,0:T(8,128)(2,1)S(1)}, u32[]{:S(2)}, u32[]{:S(2)}) %collective-permute-start.14) | collective-permute-done | bytes 196640 | tf_op jit(solution)/shard_map/ppermute | solution.py:24
  182.2 0.7 constant_dynamic-update-slice_fusion
  182.9 2.6 fusion
  185.5 4.6 %fusion.2 = bf16[384,4096]{1,0:T(8,128)(2,1)} fusion(bf16[384,4096]{1,0:T(8,128)(2,1)} %constant_dynamic-update-slice_fusion, f32[4096]{0:T(1024)S(1)} %convert_element_type.100, f32[384]{0:T(512)S(1)} %add_rsqrt_fusion.2), kind=kLoop, calls=%fused_computation.10 | loop fusion | flops 6291456 | bytes 6309376 | tf_op jit(solution)/shard_map/convert_element_type | solution.py:103
  190.1 2.0 gather_fusion.1
  192.1 1.2 fusion.25
  193.3 69.8 %psum.14 = bf16[384,48]{0,1:T(8,128)(2,1)S(1)} all-reduce(bf16[384,48]{0,1:T(8,128)(2,1)S(1)} %fusion.25), channel_id=1, replica_groups=mesh['req'=32,'mlp'=16] {'mlp'}, use_global_device_ids=true, to_apply=%region_4.5 | all-reduce | flops 18432 | bytes 73728 | tf_op jit(solution)/shard_map/psum | solution.py:140
  263.4 0.9 convolution_bitcast_fusion.2
  264.3 0.9 convolution_bitcast_fusion.3
  265.2 4.7 %copy.61 = bf16[4096,2,128]{0,2,1:T(8,128)(2,1)S(1)} copy(bf16[4096,2,128]{2,1,0:T(2,128)(2,1)} %all-gather.5.cloned.1.call-done) | data formatting | bytes 4194304 | tf_op jit(solution)/shard_map/reshape | solution.py:146
  270.0 3.3 fusion.17
  274.1 3.9 multiply_reduce_fusion
  279.0 0.9 fusion.5
  279.9 0.9 fusion.22
  280.8 19.6 %all-gather.11.cloned.1.call-done = bf16[256,16,256]{0,2,1:T(8,128)(2,1)} async-done(((bf16[256,16,8]{0,2,1:T(8,128)(2,1)}), bf16[256,16,256]{0,2,1:T(8,128)(2,1)}) %all-gather.11.cloned.1.call-update) | async-done | bytes 2097168 | tf_op jit(solution)/shard_map/all_gather | solution.py:220
  300.4 4.3 convolution_convert_fusion
  305.4 29.1 %all_gather.30 = bf16[64,16,256]{2,1,0:T(8,128)(2,1)S(1)} all-gather(bf16[2,16,256]{2,1,0:T(8,128)(2,1)S(1)} %copy-done.4), channel_id=1, replica_groups=mesh['req'=32,'mlp'=16] {'req'}, dimensions={0}, use_global_device_ids=true | all-gather | bytes 540672 | tf_op jit(solution)/shard_map/all_gather | solution.py:122
  335.0 30.0 %all_gather.31 = bf16[64,16,256]{2,1,0:T(8,128)(2,1)S(1)} all-gather(bf16[2,16,256]{2,1,0:T(8,128)(2,1)S(1)} %copy-done.5), channel_id=1, replica_groups=mesh['req'=32,'mlp'=16] {'req'}, dimensions={0}, use_global_device_ids=true | all-gather | bytes 540672 | tf_op jit(solution)/shard_map/all_gather | solution.py:125
  365.8 74.3 %psum.15 = bf16[384,16]{0,1:T(8,128)(2,1)S(1)} all-reduce(f32[384,16]{0,1:T(8,128)S(1)} %fusion.26), channel_id=1, replica_groups=mesh['req'=32,'mlp'=16] {'mlp'}, use_global_device_ids=true, to_apply=%region_12.14 | all-reduce | flops 6144 | bytes 36864 | tf_op jit(solution)/shard_map/psum | solution.py:216
  440.1 0.7 fusion.49
  440.8 1.9 fusion.16
  (98 shorter events, 14.3 us)
Async XLA Ops:
  7.2 1.0 copy-start
  7.2 90.0 %copy-start.13 = (s32[1,4]{1,0:T(1,128)S(1)}, s32[1,4]{1,0:T(1,128)}, u32[]{:S(2)}) copy-start(s32[1,4]{1,0:T(1,128)} %param.34) | copy-start | bytes 52
  7.2 90.1 %copy-start.10 = (s32[1,4,8]{2,1,0:T(4,128)S(1)}, s32[1,4,8]{2,1,0:T(4,128)}, u32[]{:S(2)}) copy-start(s32[1,4,8]{2,1,0:T(4,128)} %param.35) | copy-start | bytes 388
  7.2 182.9 %all-gather.7.cloned.1.call-start = ((), (), s32[]{:S(2)}) async-start(), calls=%async_computation.2 | async-start | bytes 1622016 | tf_op jit(solution)/shard_map/all_gather | solution.py:121
  7.9 257.3 %all-gather.5.cloned.1.call-start = ((), (), s32[]{:S(2)}) async-start(), calls=%async_computation.1 | async-start | bytes 2162688 | tf_op jit(solution)/shard_map/all_gather | solution.py:142
  8.9 265.2 %all-gather.9.cloned.1.call-start = ((), (), s32[]{:S(2)}) async-start(), calls=%async_computation.3 | async-start | bytes 2162688 | tf_op jit(solution)/shard_map/all_gather | solution.py:141
  9.7 290.8 %all-gather.11.cloned.1.call-start = ((), (), s32[]{:S(2)}) async-start(), calls=%async_computation.4 | async-start | bytes 2162688 | tf_op jit(solution)/shard_map/all_gather | solution.py:220
  9.7 94.2 %collective-permute-start = (bf16[384,256]{1,0:T(8,128)(2,1)}, bf16[384,256]{1,0:T(8,128)(2,1)S(1)}, u32[]{:S(2)}, u32[]{:S(2)}) collective-permute-start(bf16[384,256]{1,0:T(8,128)(2,1)} %param.20), channel_id=1, source_target_pairs={{0,1},{1,2},{2,3},{3,4},{4,5},{5,6},{6,7},{7,8},{8,9},{9,10},{10,1... | collective-permute-start | bytes 589832 | tf_op jit(solution)/shard_map/ppermute | solution.py:24
  13.1 92.7 %collective-permute-start.1 = (bf16[384,256]{1,0:T(8,128)(2,1)}, bf16[384,256]{1,0:T(8,128)(2,1)S(1)}, u32[]{:S(2)}, u32[]{:S(2)}) collective-permute-start(bf16[384,256]{1,0:T(8,128)(2,1)} %param.20), channel_id=1, source_target_pairs={{0,15},{1,0},{2,1},{3,2},{4,3},{5,4},{6,5},{7,6},{8,7},{9,8},{10,9... | collective-permute-start | bytes 589832 | tf_op jit(solution)/shard_map/ppermute | solution.py:27
  18.9 421.9 %reduce-scatter.2.cloned.1.call-start = ((), (), s32[]{:S(2)}) async-start(), calls=%async_computation.5 | async-start | bytes 3342336 | tf_op jit(solution)/shard_map/reduce_scatter | solution.py:223
  22.5 79.7 %copy-start.8 = (f32[64]{0:T(128)}, f32[64]{0:T(128)S(1)}, u32[]{:S(2)}) copy-start(f32[64]{0:T(128)S(1)} %multiply_exponential_fusion) | copy-start | bytes 772
  25.6 74.8 %copy-start.2 = (bf16[384,256]{1,0:T(8,128)(2,1)S(1)}, bf16[384,256]{1,0:T(8,128)(2,1)}, u32[]{:S(2)}) copy-start(bf16[384,256]{1,0:T(8,128)(2,1)} %param.20) | copy-start | bytes 589828
  103.9 88.2 %copy-start.6 = (f32[384,4]{0,1:T(4,128)}, f32[384,4]{0,1:T(4,128)S(1)}, u32[]{:S(2)}) copy-start(f32[384,4]{0,1:T(4,128)S(1)} %get-tuple-element.17) | copy-start | bytes 18436
  103.9 12.4 %collective-permute-start.2 = (bf16[384,256]{1,0:T(8,128)(2,1)S(1)}, bf16[384,256]{1,0:T(8,128)(2,1)S(1)}, u32[]{:S(2)}, u32[]{:S(2)}) collective-permute-start(bf16[384,256]{1,0:T(8,128)(2,1)S(1)} %collective-permute-done), channel_id=1, source_target_pairs={{0,1},{1,2},{2,3},{3,4},{4,5},{5,6},{6,7},{7,8},{8,9},{9,10},{10,1... | collective-permute-start | bytes 589832 | tf_op jit(solution)/shard_map/ppermute | solution.py:24
  105.8 12.3 %collective-permute-start.3 = (bf16[384,256]{1,0:T(8,128)(2,1)S(1)}, bf16[384,256]{1,0:T(8,128)(2,1)S(1)}, u32[]{:S(2)}, u32[]{:S(2)}) collective-permute-start(bf16[384,256]{1,0:T(8,128)(2,1)S(1)} %collective-permute-done.1), channel_id=1, source_target_pairs={{0,15},{1,0},{2,1},{3,2},{4,3},{5,4},{6,5},{7,6},{8,7},{9,8},{10,9... | collective-permute-start | bytes 589832 | tf_op jit(solution)/shard_map/ppermute | solution.py:27
  116.3 11.6 %collective-permute-start.4 = (bf16[384,256]{1,0:T(8,128)(2,1)S(1)}, bf16[384,256]{1,0:T(8,128)(2,1)S(1)}, u32[]{:S(2)}, u32[]{:S(2)}) collective-permute-start(bf16[384,256]{1,0:T(8,128)(2,1)S(1)} %collective-permute-done.2), channel_id=1, source_target_pairs={{0,1},{1,2},{2,3},{3,4},{4,5},{5,6},{6,7},{7,8},{8,9},{9,10},{10,1... | collective-permute-start | bytes 589832 | tf_op jit(solution)/shard_map/ppermute | solution.py:24
  118.2 11.5 %collective-permute-start.5 = (bf16[384,256]{1,0:T(8,128)(2,1)S(1)}, bf16[384,256]{1,0:T(8,128)(2,1)S(1)}, u32[]{:S(2)}, u32[]{:S(2)}) collective-permute-start(bf16[384,256]{1,0:T(8,128)(2,1)S(1)} %collective-permute-done.3), channel_id=1, source_target_pairs={{0,15},{1,0},{2,1},{3,2},{4,3},{5,4},{6,5},{7,6},{8,7},{9,8},{10,9... | collective-permute-start | bytes 589832 | tf_op jit(solution)/shard_map/ppermute | solution.py:27
  127.8 10.9 %collective-permute-start.6 = (bf16[384,256]{1,0:T(8,128)(2,1)S(1)}, bf16[384,256]{1,0:T(8,128)(2,1)S(1)}, u32[]{:S(2)}, u32[]{:S(2)}) collective-permute-start(bf16[384,256]{1,0:T(8,128)(2,1)S(1)} %collective-permute-done.4), channel_id=1, source_target_pairs={{0,1},{1,2},{2,3},{3,4},{4,5},{5,6},{6,7},{7,8},{8,9},{9,10},{10,1... | collective-permute-start | bytes 589832 | tf_op jit(solution)/shard_map/ppermute | solution.py:24
  129.8 10.9 %collective-permute-start.7 = (bf16[384,256]{1,0:T(8,128)(2,1)S(1)}, bf16[384,256]{1,0:T(8,128)(2,1)S(1)}, u32[]{:S(2)}, u32[]{:S(2)}) collective-permute-start(bf16[384,256]{1,0:T(8,128)(2,1)S(1)} %collective-permute-done.5), channel_id=1, source_target_pairs={{0,15},{1,0},{2,1},{3,2},{4,3},{5,4},{6,5},{7,6},{8,7},{9,8},{10,9... | collective-permute-start | bytes 589832 | tf_op jit(solution)/shard_map/ppermute | solution.py:27
  138.7 10.9 %collective-permute-start.8 = (bf16[384,256]{1,0:T(8,128)(2,1)S(1)}, bf16[384,256]{1,0:T(8,128)(2,1)S(1)}, u32[]{:S(2)}, u32[]{:S(2)}) collective-permute-start(bf16[384,256]{1,0:T(8,128)(2,1)S(1)} %collective-permute-done.6), channel_id=1, source_target_pairs={{0,1},{1,2},{2,3},{3,4},{4,5},{5,6},{6,7},{7,8},{8,9},{9,10},{10,1... | collective-permute-start | bytes 589832 | tf_op jit(solution)/shard_map/ppermute | solution.py:24
  140.6 10.9 %collective-permute-start.9 = (bf16[384,256]{1,0:T(8,128)(2,1)S(1)}, bf16[384,256]{1,0:T(8,128)(2,1)S(1)}, u32[]{:S(2)}, u32[]{:S(2)}) collective-permute-start(bf16[384,256]{1,0:T(8,128)(2,1)S(1)} %collective-permute-done.7), channel_id=1, source_target_pairs={{0,15},{1,0},{2,1},{3,2},{4,3},{5,4},{6,5},{7,6},{8,7},{9,8},{10,9... | collective-permute-start | bytes 589832 | tf_op jit(solution)/shard_map/ppermute | solution.py:27
  149.6 10.9 %collective-permute-start.10 = (bf16[384,256]{1,0:T(8,128)(2,1)S(1)}, bf16[384,256]{1,0:T(8,128)(2,1)S(1)}, u32[]{:S(2)}, u32[]{:S(2)}) collective-permute-start(bf16[384,256]{1,0:T(8,128)(2,1)S(1)} %collective-permute-done.8), channel_id=1, source_target_pairs={{0,1},{1,2},{2,3},{3,4},{4,5},{5,6},{6,7},{7,8},{8,9},{9,10},{10,1... | collective-permute-start | bytes 589832 | tf_op jit(solution)/shard_map/ppermute | solution.py:24
  151.5 10.9 %collective-permute-start.11 = (bf16[384,256]{1,0:T(8,128)(2,1)S(1)}, bf16[384,256]{1,0:T(8,128)(2,1)S(1)}, u32[]{:S(2)}, u32[]{:S(2)}) collective-permute-start(bf16[384,256]{1,0:T(8,128)(2,1)S(1)} %collective-permute-done.9), channel_id=1, source_target_pairs={{0,15},{1,0},{2,1},{3,2},{4,3},{5,4},{6,5},{7,6},{8,7},{9,8},{10,9... | collective-permute-start | bytes 589832 | tf_op jit(solution)/shard_map/ppermute | solution.py:27
  160.4 10.9 %collective-permute-start.12 = (bf16[384,256]{1,0:T(8,128)(2,1)S(1)}, bf16[384,256]{1,0:T(8,128)(2,1)S(1)}, u32[]{:S(2)}, u32[]{:S(2)}) collective-permute-start(bf16[384,256]{1,0:T(8,128)(2,1)S(1)} %collective-permute-done.10), channel_id=1, source_target_pairs={{0,1},{1,2},{2,3},{3,4},{4,5},{5,6},{6,7},{7,8},{8,9},{9,10},{10,1... | collective-permute-start | bytes 589832 | tf_op jit(solution)/shard_map/ppermute | solution.py:24
  162.4 11.6 %collective-permute-start.13 = (bf16[384,256]{1,0:T(8,128)(2,1)S(1)}, bf16[384,256]{1,0:T(8,128)(2,1)S(1)}, u32[]{:S(2)}, u32[]{:S(2)}) collective-permute-start(bf16[384,256]{1,0:T(8,128)(2,1)S(1)} %collective-permute-done.11), channel_id=1, source_target_pairs={{0,15},{1,0},{2,1},{3,2},{4,3},{5,4},{6,5},{7,6},{8,7},{9,8},{10,9... | collective-permute-start | bytes 589832 | tf_op jit(solution)/shard_map/ppermute | solution.py:27
  171.3 10.9 %collective-permute-start.14 = (bf16[384,256]{1,0:T(8,128)(2,1)S(1)}, bf16[384,256]{1,0:T(8,128)(2,1)S(1)}, u32[]{:S(2)}, u32[]{:S(2)}) collective-permute-start(bf16[384,256]{1,0:T(8,128)(2,1)S(1)} %collective-permute-done.12), channel_id=1, source_target_pairs={{0,1},{1,2},{2,3},{3,4},{4,5},{5,6},{6,7},{7,8},{8,9},{9,10},{10,1... | collective-permute-start | bytes 589832 | tf_op jit(solution)/shard_map/ppermute | solution.py:24
  270.0 3.4 copy-start.11
  270.0 3.5 copy-start.9
  274.1 4.2 copy-start.12
  278.0 1.0 copy-start.1
  278.5 1.4 copy-start.3
  304.7 0.7 copy-start.4
  304.7 30.3 %copy-start.5 = (bf16[2,16,256]{2,1,0:T(8,128)(2,1)S(1)}, bf16[2,16,256]{2,1,0:T(8,128)(2,1)}, u32[]{:S(2)}) copy-start(bf16[2,16,256]{2,1,0:T(8,128)(2,1)} %param.31) | copy-start | bytes 49156
  304.7 60.9 %copy-start.7 = (f32[384,4]{0,1:T(4,128)S(1)}, f32[384,4]{0,1:T(4,128)}, u32[]{:S(2)}) copy-start(f32[384,4]{0,1:T(4,128)} %copy-done.6) | copy-start | bytes 18436
Sparse Core Ops, SparseCore 0:
  10.2 75.4 all-gather.6
  88.4 68.8 all-gather.4
  159.4 68.7 all-gather.8
  230.1 70.2 all-gather.10
  304.8 87.2 reduce-scatter.1
